TPU v7x, 32 devices: a whole 2x2x4 slice. The times are simulated.
32 devices in a mesh: groups: 2 (over y), out: 4 (over z), inp: 4 (over x, core).
Axes of the slice: x: 2, y: 2, z: 4, core: 2. Of those that a mesh axis runs over, the one named last changes fastest.
Arguments:
- acts_rot: bfloat16 [64, 8192], P(('groups', 'out', 'inp')), parts along dimension 0, may hold values from -6 to 6
- grads_rot: bfloat16 [64, 28672], P(('groups', 'out', 'inp')), parts along dimension 0, may hold values from -0.00024414062 to 0.00024414062
- query_grads: bfloat16 [8, 128, 28672], P('groups', None, 'out'), parts along dimension 0, may hold values from -6 to 6
- query_acts: bfloat16 [8, 128, 8192], P('groups', 'out', 'inp'), parts along dimension 0, may hold values from -0.5 to 0.5
- eigen: bfloat16 [28672, 8192], P('out', 'inp'), may hold values from 0.049804688 to 5
- block_mask: int32 [8, 224, 64], P('groups'), parts along dimension 0, may hold values from 0 to 1, as said below
- order: int32 [64], P('groups'), parts along dimension 0, may hold values from 0 to 31, each once
- segment_ids: int32 [64], P('groups'), parts along dimension 0, may hold values from 0 to 3, never falling along the last dimension, each value on 1 to 16 neighbouring positions
Outputs:
- token_scores: float32 [4, 64], P(None, 'groups'), parts along dimension 1
- seq_scores: float32 [8, 4], P('groups'), parts along dimension 0
There are 2 independent parts, one for each index of `groups`. A program takes and returns all parts, laid end to end along the dimension named above; an argument that names none is the same for every part. Nothing has to cross between parts.
Inputs may be any that keep to these rules, and one draw needn't show every extreme that they name: block_mask[q, r, c] is 1 where query q keeps the block of rows r * 128 to r * 128 + 127 and columns c * 128 to c * 128 + 127, else 0. order holds each of the 32 positions once. segment_ids never falls along the positions; each sequence has 1 to 16 positions and one has exactly 16.
All inputs are finite; a program needn't handle non-finite values.
Results may differ from a plain program's by a relative error of at most 0.0035.
Values may be sent and summed in bfloat16 or wider, within the bound.
No kernel may reach another device: no remote copies, remote signals or barrier semaphores. Data moves between devices by JAX's collectives and lax.ppermute only.
A program may use at most 512 MiB of HBM per device.

v0:
```python
import jax
import jax.numpy as jnp
from jax import lax
from jax.sharding import PartitionSpec as P

BLOCK = 128
SEQS = 4
damping = 0.1


def per_device(acts_rot, grads_rot, query_grads, query_acts, eigen, block_mask, order, segment_ids):
    row_count, col_count = eigen.shape
    queries = block_mask.shape[0]
    total_blocks = block_mask.shape[1]
    col_blocks = col_count // BLOCK
    span = row_count // BLOCK + 2
    row_offset = lax.axis_index("out") * row_count
    col_offset = lax.axis_index("inp") * col_count
    first_block = jnp.minimum(row_offset // BLOCK, total_blocks - span)
    mask_band = lax.dynamic_slice(
        block_mask, (jnp.int32(0), first_block, col_offset // BLOCK), (queries, span, col_blocks)
    ).astype(jnp.float32)
    local_block = (row_offset + jnp.arange(row_count, dtype=jnp.int32)) // BLOCK - first_block
    row_pick = (local_block[:, None] == jnp.arange(span, dtype=jnp.int32)[None, :]).astype(
        jnp.float32
    )
    mask_rows = (
        jnp.einsum("rs,qsc->qrc", row_pick, mask_band, precision=lax.Precision.HIGHEST) > 0.5
    )
    query_whole = lax.all_gather(query_acts, "out", axis=1, tiled=True)
    outer_sum = jnp.einsum(
        "qsi,qsj->qij", query_grads, query_whole, preferred_element_type=jnp.float32
    )
    scaled = outer_sum / (eigen.astype(jnp.float32) + damping)[None]
    scaled = scaled.reshape(queries, row_count, col_blocks, BLOCK)
    precond = (
        jnp.where(mask_rows[..., None], scaled, 0.0)
        .astype(jnp.bfloat16)
        .reshape(queries, row_count, col_count)
    )
    spread = lax.all_to_all(grads_rot[None], "out", split_axis=2, concat_axis=0, tiled=True)
    grad_cols = lax.all_gather(spread, "inp", axis=1, tiled=True).reshape(-1, row_count)
    whole_rows = lax.all_gather(acts_rot, ("out", "inp"), axis=0, tiled=True)
    token_cols = lax.dynamic_slice_in_dim(whole_rows, col_offset, col_count, 1)
    grad_float = grad_cols.astype(jnp.float32)
    partial_rows = []
    for query_index in range(queries):
        image = lax.dot_general(
            token_cols,
            precond[query_index],
            (((1,), (1,)), ((), ())),
            preferred_element_type=jnp.float32,
        )
        partial_rows.append(jnp.sum(image * grad_float, axis=1))
    partial_value = jnp.stack(partial_rows, axis=0)
    score_total = lax.psum(partial_value, ("out", "inp"))
    token_scores = jnp.zeros_like(score_total).at[:, order].set(score_total)
    member = (segment_ids[:, None] == jnp.arange(SEQS, dtype=jnp.int32)[None, :]).astype(
        jnp.float32
    )
    seq_scores = jnp.dot(token_scores, member, precision=lax.Precision.HIGHEST)
    return (token_scores, seq_scores)


def solution(mesh):
    in_specs = (
        P(("groups", "out", "inp"), None),
        P(("groups", "out", "inp"), None),
        P("groups", None, "out"),
        P("groups", "out", "inp"),
        P("out", "inp"),
        P("groups", None, None),
        P("groups"),
        P("groups"),
    )
    out_specs = (P(None, "groups"), P("groups", None))
    return jax.shard_map(
        per_device, mesh=mesh, in_specs=in_specs, out_specs=out_specs, check_vma=False
    )
```

profile of v0, /device:TPU:0, one launch (start us, length us, event | category | flops | bytes accessed | tf_op | source)
XLA Modules:
  0.0 682.6 jit_solution(16952573298580868465)
XLA Ops:
  7.2 0.0 all-gather.4.cloned.1.call-start
  7.2 0.7 all-gather.4.cloned.1.call-update
  7.9 25.8 %copy.28 = bf16[1,2,28672]{1,0,2:T(2,128)(2,1)} copy(bf16[1,2,28672]{2,1,0:T(2,128)(2,1)} %bitcast.42) | data formatting | bytes 229376 | tf_op jit(solution)/shard_map/broadcast_in_dim | solution.py:41
  33.7 0.5 broadcast.49
  34.2 157.1 %reduce = bf16[28672,2]{1,0:T(8,128)(2,1)} reduce(bf16[28672,1,2]{2,1,0:T(2,128)(2,1)} %bitcast.39, bf16[]{:T(256)} %broadcast.49), dimensions={1}, to_apply=%bitcast.26.reduce_sub_computation | reduce | bytes 229378
  191.3 14.9 %reshape.61 = bf16[4,2,7168]{2,1,0:T(2,128)(2,1)} reshape(bf16[28672,2]{1,0:T(8,128)(2,1)} %reduce) | data formatting | bytes 229376
  206.2 6.3 all-to-all-start
  212.6 28.3 %convert_add_fusion = f32[7168,2048]{1,0:T(8,128)} fusion(bf16[7168,2048]{1,0:T(8,128)(2,1)} %param.12), kind=kLoop, calls=%fused_computation.3 | loop fusion | flops 29360128 | bytes 88080384 | tf_op jit(solution)/shard_map/add | solution.py:34
  240.9 53.6 %copy.27 = f32[7168,2048]{0,1:T(8,128)} copy(f32[7168,2048]{1,0:T(8,128)} %convert_add_fusion) | data formatting | bytes 117440512 | tf_op jit(solution)/shard_map/add | solution.py:34
  294.5 23.6 %all-gather.1 = bf16[16,2,8192]{2,1,0:T(2,128)(2,1)S(1)} all-gather(bf16[1,2,8192]{2,1,0:T(2,128)(2,1)S(1)} %bitcast.43), channel_id=1, replica_groups=mesh['groups'=2,'out'=4,'inp'=4] {'out','inp'}, dimensions={0}, use_global_device_ids=true | all-gather | bytes 557056 | tf_op jit(solution)/shard_map/all_gather | solution.py:43
  318.1 1.0 reshape.57
  319.1 2.7 fusion
  321.9 0.5 compare_select_fusion
  322.4 0.0 all-to-all-done
  322.4 18.2 %reshape.62 = bf16[28672,1,2]{2,1,0:T(2,128)(2,1)} reshape(bf16[4,2,7168]{2,1,0:T(2,128)(2,1)S(1)} %all-to-all-done) | data formatting | bytes 229376
  340.6 26.8 %copy.29 = bf16[1,2,28672]{2,1,0:T(2,128)(2,1)S(1)} copy(bf16[1,2,28672]{1,0,2:T(2,128)(2,1)} %bitcast.40) | data formatting | bytes 229376 | tf_op jit(solution)/shard_map/all_to_all | solution.py:41
  367.4 0.1 all_to_all.14
  367.5 7.4 %all-gather = bf16[4,1,8,7168]{3,0,1,2:T(4,128)(2,1)} all-gather(bf16[4,1,2,7168]{3,0,1,2:T(4,128)(2,1)S(1)} %bitcast.41), channel_id=2, replica_groups=mesh['groups'=2,'out'=4,'inp'=4] {'inp'}, dimensions={2}, use_global_device_ids=true | all-gather | bytes 573440 | tf_op jit(solution)/shard_map/all_gather | solution.py:42
  374.9 65.7 %broadcast_divide_fusion = bf16[4,7168,2048]{1,2,0:T(8,128)(2,1)} fusion(f32[7168,2048]{0,1:T(8,128)} %copy.27, bf16[4,128,7168]{2,1,0:T(8,128)(2,1)} %param.10, bf16[4,128,2048]{2,1,0:T(8,128)(2,1)} %all-gather.4.cloned.1.call-done), kind=kOutput, calls=%fused_computation.2 | convolution fusion | flops 15149826048 | bytes 185597952 | tf_op jit(solution)/shard_map/qsi,qsj->qij/dot_general | solution.py:31
  440.6 76.5 %select_convert_fusion = bf16[4,7168,16,128]{1,3,2,0:T(8,128)(2,1)} fusion(bf16[4,7168,16,128]{1,3,2,0:T(8,128)(2,1)} %bitcast.3, pred[4,7168,16]{1,2,0:T(8,128)(4,1)S(1)} %copy-done.2), kind=kLoop, calls=%fused_computation.1 | loop fusion | flops 58720256 | bytes 235339776 | tf_op jit(solution)/shard_map/convert_element_type | solution.py:38
  517.1 77.2 %fusion.27 = (bf16[1,7168,16,128]{1,3,2,0:T(8,128)(2,1)}, bf16[1,7168,16,128]{1,3,2,0:T(8,128)(2,1)}, bf16[1,7168,16,128]{1,3,2,0:T(8,128)(2,1)}, bf16[1,7168,16,128]{1,3,2,0:T(8,128)(2,1)}) fusion(bf16[4,7168,16,128]{1,3,2,0:T(8,128)(2,1)} %select_convert_fusion), kind=kLoop, calls=%fused_computation.45 | loop fusion | bytes 234881024 | tf_op jit(solution)/shard_map/slice | solution.py:50
  594.3 12.3 %fusion.3 = f32[32]{0:T(128)S(1)} fusion(bf16[7168,2048]{0,1:T(8,128)(2,1)} %bitcast.38, bf16[4,1,8,7168]{3,0,1,2:T(4,128)(2,1)S(1)} %copy-done, bf16[32,8192]{1,0:T(8,128)(2,1)S(1)} %copy-done.1, s32[]{:T(128)S(6)} %select_n.34), kind=kOutput, calls=%fused_computation.12 | convolution fusion | flops 940212224 | bytes 29950084 | tf_op jit(solution)/shard_map/dot_general | solution.py:48
  606.6 12.3 %fusion.4 = f32[32]{0:T(128)S(1)} fusion(bf16[7168,2048]{0,1:T(8,128)(2,1)} %bitcast.37, bf16[4,1,8,7168]{3,0,1,2:T(4,128)(2,1)S(1)} %copy-done, bf16[32,8192]{1,0:T(8,128)(2,1)S(1)} %copy-done.1, s32[]{:T(128)S(6)} %select_n.34), kind=kOutput, calls=%fused_computation.13 | convolution fusion | flops 940212224 | bytes 29950084 | tf_op jit(solution)/shard_map/dot_general | solution.py:48
  618.9 0.0 copy-start.5
  618.9 12.3 %fusion.5 = f32[32]{0:T(128)S(1)} fusion(bf16[7168,2048]{0,1:T(8,128)(2,1)} %bitcast.36, bf16[4,1,8,7168]{3,0,1,2:T(4,128)(2,1)S(1)} %copy-done, bf16[32,8192]{1,0:T(8,128)(2,1)S(1)} %copy-done.1, s32[]{:T(128)S(6)} %select_n.34), kind=kOutput, calls=%fused_computation.14 | convolution fusion | flops 940212224 | bytes 29950084 | tf_op jit(solution)/shard_map/dot_general | solution.py:48
  631.2 12.5 %fusion.6 = f32[32]{0:T(128)S(1)} fusion(bf16[7168,2048]{0,1:T(8,128)(2,1)} %bitcast.35, bf16[4,1,8,7168]{3,0,1,2:T(4,128)(2,1)S(1)} %copy-done, bf16[32,8192]{1,0:T(8,128)(2,1)S(1)} %copy-done.1, s32[]{:T(128)S(6)} %select_n.34), kind=kOutput, calls=%fused_computation.15 | convolution fusion | flops 940212224 | bytes 29950084 | tf_op jit(solution)/shard_map/dot_general | solution.py:48
  643.7 29.8 %psum.7 = f32[4,32]{1,0:T(4,128)S(1)} all-reduce(f32[4,32]{1,0:T(4,128)S(1)} %pad_maximum_fusion), channel_id=1, replica_groups=mesh['groups'=2,'out'=4,'inp'=4] {'out','inp'}, use_global_device_ids=true, to_apply=%region_4.5 | all-reduce | flops 128 | bytes 1024 | tf_op jit(solution)/shard_map/psum | solution.py:56
  673.5 0.1 copy.32
  673.6 0.8 scatter_custom_fusion
  674.4 0.7 copy.33
  675.0 0.0 copy-done.5
  675.0 0.8 fusion.18
  (13 shorter events, 0.1 us)
Async XLA Ops:
  7.2 367.7 %all-gather.4.cloned.1.call-start = ((), (), s32[]{:S(2)}) async-start(), calls=%async_computation.1 | async-start | bytes 2621440 | tf_op jit(solution)/shard_map/all_gather | solution.py:30
  206.2 116.2 %all-to-all-start = ((bf16[4,2,7168]{2,1,0:T(2,128)(2,1)}), bf16[4,2,7168]{2,1,0:T(2,128)(2,1)S(1)}, u32[]{:S(2)}, u32[]{:S(2)}) async-start(bf16[4,2,7168]{2,1,0:T(2,128)(2,1)} %reshape.61), calls=%async_computation | async-start | bytes 229376 | tf_op jit(solution)/shard_map/all_to_all | solution.py:41
  240.9 53.6 %copy-start.3 = (bf16[2,8192]{1,0:T(2,128)(2,1)S(1)}, bf16[2,8192]{1,0:T(2,128)(2,1)}, u32[]{:S(2)}) copy-start(bf16[2,8192]{1,0:T(2,128)(2,1)} %param.8) | copy-start | bytes 98308
  240.9 81.0 %copy-start.4 = (s32[32]{0:T(128)S(1)}, s32[32]{0:T(128)}, u32[]{:S(2)}) copy-start(s32[32]{0:T(128)} %param.14) | copy-start | bytes 388
  374.9 65.7 %copy-start.2 = (pred[4,7168,16]{1,2,0:T(8,128)(4,1)S(1)}, pred[4,7168,16]{1,2,0:T(8,128)(4,1)}, u32[]{:S(2)}) copy-start(pred[4,7168,16]{1,2,0:T(8,128)(4,1)} %fusion) | copy-start | bytes 1376260
  517.1 77.2 %copy-start = (bf16[4,1,8,7168]{3,0,1,2:T(4,128)(2,1)S(1)}, bf16[4,1,8,7168]{3,0,1,2:T(4,128)(2,1)}, u32[]{:S(2)}) copy-start(bf16[4,1,8,7168]{3,0,1,2:T(4,128)(2,1)} %all-gather) | copy-start | bytes 1376260
  517.1 77.2 %copy-start.1 = (bf16[32,8192]{1,0:T(8,128)(2,1)S(1)}, bf16[32,8192]{1,0:T(8,128)(2,1)}, u32[]{:S(2)}) copy-start(bf16[32,8192]{1,0:T(8,128)(2,1)} %reshape.57) | copy-start | bytes 1572868
  618.9 56.2 %copy-start.5 = (s32[32]{0:T(128)S(1)}, s32[32]{0:T(128)}, u32[]{:S(2)}) copy-start(s32[32]{0:T(128)} %param.15) | copy-start | bytes 388
Sparse Core Ops, SparseCore 0:
  9.5 48.3 all-gather.3
where the time goes:
time: 685 us; the launch traced here: 683 us
  other arithmetic  262 us (38%)
  local copies, waits for them, and re-layouts  220 us (32%)
  matrix products  119 us (17%)
  blocking collectives  60.8 us (9%)
  between operations  14.1 us (2%)
    unnamed x1, other arithmetic  157 us
    slice x1, local copies, waits for them, and re-layouts, per_device(): precond[query_index]  77.2 us
    convert_element_type x1, other arithmetic, per_device(): precond = jnp.where(mask_rows[..., None], scaled, 0.0).astype(jnp.bfloat1...  76.5 us
    dot_general x1, matrix products, per_device(): jnp.einsum('qsi,qsj->qij', query_grads, query_whole, preferred_element_ty...  65.7 us
    add x1, local copies, waits for them, and re-layouts, per_device(): scaled = outer_sum / (eigen.astype(jnp.float32) + damping)[None]  53.6 us
    dot_general x4, matrix products, per_device(): lax.dot_general(token_cols, precond[query_index], (((1,), (1,)), ((), ())...  49.4 us
    unnamed x17, local copies, waits for them, and re-layouts  35.3 us
    psum x1, blocking collectives, per_device(): score_total = lax.psum(partial_value, ('out', 'inp'))  29.8 us
  transfers between devices with their start and end apart: 2, of which 0 were waited for; matrix products, arithmetic and copies ran while one was open for 48% of the time, Pallas kernels for 0%

commit v1 on v0

--- a/solution.py
+++ b/solution.py
@@ -38,7 +38,12 @@
         .astype(jnp.bfloat16)
         .reshape(queries, row_count, col_count)
     )
-    spread = lax.all_to_all(grads_rot[None], "out", split_axis=2, concat_axis=0, tiled=True)
+    spread = jnp.concatenate(
+        lax.all_to_all(
+            jnp.stack(jnp.split(grads_rot[None], lax.axis_size("out"), axis=2)), "out", 0, 0
+        ),
+        axis=0,
+    )
     grad_cols = lax.all_gather(spread, "inp", axis=1, tiled=True).reshape(-1, row_count)
     whole_rows = lax.all_gather(acts_rot, ("out", "inp"), axis=0, tiled=True)
     token_cols = lax.dynamic_slice_in_dim(whole_rows, col_offset, col_count, 1)

time: 685 us -> 443 us (0.65)
  other arithmetic: 262 us -> 107 us
  local copies, waits for them, and re-layouts: 220 us -> 134 us
    unnamed x1 -> x0, other arithmetic: 157 us -> none
    unnamed x17 -> x14, local copies, waits for them, and re-layouts: 35.3 us -> 1.69 us
    all_to_all x2 -> x1, local copies, waits for them, and re-layouts: 26.9 us -> 0.05 us  [per_device(): lax.all_to_all(jnp.stack(jnp.split(grads_rot[None], lax.axis_size('out'),...]
    broadcast_in_dim x1 -> x0, local copies, waits for them, and re-layouts: 25.8 us -> none  [per_device(): grads_rot[None]]
  transfers between devices with their start and end apart: 2 -> 2, of which waited for: 0 -> 0; matrix products, arithmetic and copies ran while one was open for 48% -> 20% of each run, Pallas kernels for 0% -> 0%
where the time goes in v1:
time: 443 us; the launch traced here: 442 us
  local copies, waits for them, and re-layouts  134 us (30%)
  matrix products  119 us (27%)
  other arithmetic  107 us (24%)
  blocking collectives  60.8 us (14%)
  between operations  14.1 us (3%)
  starting transfers between devices  6.38 us (1%)
    slice x1, local copies, waits for them, and re-layouts, per_device(): precond[query_index]  77.2 us
    convert_element_type x1, other arithmetic, per_device(): precond = jnp.where(mask_rows[..., None], scaled, 0.0).astype(jnp.bfloat1...  76.5 us
    dot_general x1, matrix products, per_device(): jnp.einsum('qsi,qsj->qij', query_grads, query_whole, preferred_element_ty...  65.7 us
    add x1, local copies, waits for them, and re-layouts, per_device(): scaled = outer_sum / (eigen.astype(jnp.float32) + damping)[None]  53.6 us
    dot_general x4, matrix products, per_device(): lax.dot_general(token_cols, precond[query_index], (((1,), (1,)), ((), ())...  49.4 us
    psum x1, blocking collectives, per_device(): score_total = lax.psum(partial_value, ('out', 'inp'))  29.8 us
    add x1, other arithmetic, per_device(): scaled = outer_sum / (eigen.astype(jnp.float32) + damping)[None]  28.8 us
    all_gather x1, blocking collectives, per_device(): whole_rows = lax.all_gather(acts_rot, ('out', 'inp'), axis=0, tiled=True)  23.4 us
  transfers between devices with their start and end apart: 2, of which 0 were waited for; matrix products, arithmetic and copies ran while one was open for 20% of the time, Pallas kernels for 0%

profile of v1, /device:TPU:0, one launch (start us, length us, event | category | flops | bytes accessed | tf_op | source)
XLA Modules:
  0.0 441.5 jit_solution(7068360197900982658)
XLA Ops:
  7.2 0.0 all-gather.4.cloned.1.call-start
  7.2 0.7 all-gather.4.cloned.1.call-update
  7.9 0.9 slice_bitcast_fusion.3
  8.8 0.8 pad_maximum_fusion
  9.6 6.3 %all-to-all-start = ((bf16[4,1,2,7168]{3,2,1,0:T(2,128)(2,1)}), bf16[4,1,2,7168]{3,2,1,0:T(2,128)(2,1)S(1)}, u32[]{:S(2)}, u32[]{:S(2)}) async-start(bf16[4,1,2,7168]{3,2,1,0:T(2,128)(2,1)} %pad_maximum_fusion), calls=%async_computation | async-start | bytes 229376 | tf_op jit(solution)/shard_map/all_to_all | solution.py:42
  16.0 28.8 %convert_add_fusion = f32[7168,2048]{1,0:T(8,128)} fusion(bf16[7168,2048]{1,0:T(8,128)(2,1)} %param.12), kind=kLoop, calls=%fused_computation.3 | loop fusion | flops 29360128 | bytes 88080384 | tf_op jit(solution)/shard_map/add | solution.py:34
  44.8 53.6 %copy.25 = f32[7168,2048]{0,1:T(8,128)} copy(f32[7168,2048]{1,0:T(8,128)} %convert_add_fusion) | data formatting | bytes 117440512 | tf_op jit(solution)/shard_map/add | solution.py:34
  98.4 0.0 copy-done.3
  98.5 23.4 %all-gather.1 = bf16[16,2,8192]{2,1,0:T(2,128)(2,1)S(1)} all-gather(bf16[1,2,8192]{2,1,0:T(2,128)(2,1)S(1)} %bitcast.43), channel_id=1, replica_groups=mesh['groups'=2,'out'=4,'inp'=4] {'out','inp'}, dimensions={0}, use_global_device_ids=true | all-gather | bytes 557056 | tf_op jit(solution)/shard_map/all_gather | solution.py:48
  121.9 1.0 reshape.61
  122.9 2.8 fusion
  125.7 0.0 copy-done.4
  125.7 0.5 compare_select_fusion
  126.2 0.0 all-to-all-done
  126.2 7.6 %all-gather = bf16[4,1,8,7168]{3,0,1,2:T(4,128)(2,1)} all-gather(bf16[4,1,2,7168]{3,0,1,2:T(4,128)(2,1)S(1)} %copy.26), channel_id=2, replica_groups=mesh['groups'=2,'out'=4,'inp'=4] {'inp'}, dimensions={2}, use_global_device_ids=true | all-gather | bytes 573440 | tf_op jit(solution)/shard_map/all_gather | solution.py:47
  133.8 65.7 %broadcast_divide_fusion = bf16[4,7168,2048]{1,2,0:T(8,128)(2,1)} fusion(f32[7168,2048]{0,1:T(8,128)} %copy.25, bf16[4,128,7168]{2,1,0:T(8,128)(2,1)} %param.10, bf16[4,128,2048]{2,1,0:T(8,128)(2,1)} %all-gather.4.cloned.1.call-done), kind=kOutput, calls=%fused_computation.2 | convolution fusion | flops 15149826048 | bytes 185597952 | tf_op jit(solution)/shard_map/qsi,qsj->qij/dot_general | solution.py:31
  199.5 0.0 copy-done.2
  199.5 76.5 %select_convert_fusion = bf16[4,7168,16,128]{1,3,2,0:T(8,128)(2,1)} fusion(bf16[4,7168,16,128]{1,3,2,0:T(8,128)(2,1)} %bitcast.3, pred[4,7168,16]{1,2,0:T(8,128)(4,1)S(1)} %copy-done.2), kind=kLoop, calls=%fused_computation.1 | loop fusion | flops 58720256 | bytes 235339776 | tf_op jit(solution)/shard_map/convert_element_type | solution.py:38
  276.0 77.2 %fusion.27 = (bf16[1,7168,16,128]{1,3,2,0:T(8,128)(2,1)}, bf16[1,7168,16,128]{1,3,2,0:T(8,128)(2,1)}, bf16[1,7168,16,128]{1,3,2,0:T(8,128)(2,1)}, bf16[1,7168,16,128]{1,3,2,0:T(8,128)(2,1)}) fusion(bf16[4,7168,16,128]{1,3,2,0:T(8,128)(2,1)} %select_convert_fusion), kind=kLoop, calls=%fused_computation.50 | loop fusion | bytes 234881024 | tf_op jit(solution)/shard_map/slice | solution.py:55
  353.1 0.0 copy-done
  353.1 0.0 copy-done.1
  353.1 12.3 %fusion.3 = f32[32]{0:T(128)S(1)} fusion(bf16[7168,2048]{0,1:T(8,128)(2,1)} %bitcast.41, bf16[4,1,8,7168]{3,0,1,2:T(4,128)(2,1)S(1)} %copy-done, bf16[32,8192]{1,0:T(8,128)(2,1)S(1)} %copy-done.1, s32[]{:T(128)S(6)} %select_n.34), kind=kOutput, calls=%fused_computation.12 | convolution fusion | flops 940212224 | bytes 29950084 | tf_op jit(solution)/shard_map/dot_general | solution.py:53
  365.4 12.3 %fusion.4 = f32[32]{0:T(128)S(1)} fusion(bf16[7168,2048]{0,1:T(8,128)(2,1)} %bitcast.40, bf16[4,1,8,7168]{3,0,1,2:T(4,128)(2,1)S(1)} %copy-done, bf16[32,8192]{1,0:T(8,128)(2,1)S(1)} %copy-done.1, s32[]{:T(128)S(6)} %select_n.34), kind=kOutput, calls=%fused_computation.13 | convolution fusion | flops 940212224 | bytes 29950084 | tf_op jit(solution)/shard_map/dot_general | solution.py:53
  377.7 0.0 copy-start.5
  377.7 12.3 %fusion.5 = f32[32]{0:T(128)S(1)} fusion(bf16[7168,2048]{0,1:T(8,128)(2,1)} %bitcast.39, bf16[4,1,8,7168]{3,0,1,2:T(4,128)(2,1)S(1)} %copy-done, bf16[32,8192]{1,0:T(8,128)(2,1)S(1)} %copy-done.1, s32[]{:T(128)S(6)} %select_n.34), kind=kOutput, calls=%fused_computation.14 | convolution fusion | flops 940212224 | bytes 29950084 | tf_op jit(solution)/shard_map/dot_general | solution.py:53
  390.0 12.5 %fusion.6 = f32[32]{0:T(128)S(1)} fusion(bf16[7168,2048]{0,1:T(8,128)(2,1)} %bitcast.38, bf16[4,1,8,7168]{3,0,1,2:T(4,128)(2,1)S(1)} %copy-done, bf16[32,8192]{1,0:T(8,128)(2,1)S(1)} %copy-done.1, s32[]{:T(128)S(6)} %select_n.34), kind=kOutput, calls=%fused_computation.15 | convolution fusion | flops 940212224 | bytes 29950084 | tf_op jit(solution)/shard_map/dot_general | solution.py:53
  402.5 29.8 %psum.7 = f32[4,32]{1,0:T(4,128)S(1)} all-reduce(f32[4,32]{1,0:T(4,128)S(1)} %pad_maximum_fusion.1), channel_id=1, replica_groups=mesh['groups'=2,'out'=4,'inp'=4] {'out','inp'}, use_global_device_ids=true, to_apply=%region_4.5 | all-reduce | flops 128 | bytes 1024 | tf_op jit(solution)/shard_map/psum | solution.py:61
  432.4 0.1 copy.28
  432.5 0.8 scatter_custom_fusion
  433.3 0.7 copy.29
  433.9 0.0 copy-done.5
  433.9 0.8 fusion.18
  (9 shorter events, 0.1 us)
Async XLA Ops:
  7.2 126.6 %all-gather.4.cloned.1.call-start = ((), (), s32[]{:S(2)}) async-start(), calls=%async_computation.1 | async-start | bytes 2621440 | tf_op jit(solution)/shard_map/all_gather | solution.py:30
  9.6 116.6 %all-to-all-start = ((bf16[4,1,2,7168]{3,2,1,0:T(2,128)(2,1)}), bf16[4,1,2,7168]{3,2,1,0:T(2,128)(2,1)S(1)}, u32[]{:S(2)}, u32[]{:S(2)}) async-start(bf16[4,1,2,7168]{3,2,1,0:T(2,128)(2,1)} %pad_maximum_fusion), calls=%async_computation | async-start | bytes 229376 | tf_op jit(solution)/shard_map/all_to_all | solution.py:42
  44.8 53.6 %copy-start.3 = (bf16[2,8192]{1,0:T(2,128)(2,1)S(1)}, bf16[2,8192]{1,0:T(2,128)(2,1)}, u32[]{:S(2)}) copy-start(bf16[2,8192]{1,0:T(2,128)(2,1)} %param.8) | copy-start | bytes 98308
  44.8 80.8 %copy-start.4 = (s32[32]{0:T(128)S(1)}, s32[32]{0:T(128)}, u32[]{:S(2)}) copy-start(s32[32]{0:T(128)} %param.14) | copy-start | bytes 388
  133.8 65.7 %copy-start.2 = (pred[4,7168,16]{1,2,0:T(8,128)(4,1)S(1)}, pred[4,7168,16]{1,2,0:T(8,128)(4,1)}, u32[]{:S(2)}) copy-start(pred[4,7168,16]{1,2,0:T(8,128)(4,1)} %fusion) | copy-start | bytes 1376260
  275.9 77.2 %copy-start = (bf16[4,1,8,7168]{3,0,1,2:T(4,128)(2,1)S(1)}, bf16[4,1,8,7168]{3,0,1,2:T(4,128)(2,1)}, u32[]{:S(2)}) copy-start(bf16[4,1,8,7168]{3,0,1,2:T(4,128)(2,1)} %all-gather) | copy-start | bytes 1376260
  275.9 77.2 %copy-start.1 = (bf16[32,8192]{1,0:T(8,128)(2,1)S(1)}, bf16[32,8192]{1,0:T(8,128)(2,1)}, u32[]{:S(2)}) copy-start(bf16[32,8192]{1,0:T(8,128)(2,1)} %reshape.61) | copy-start | bytes 1572868
  377.7 56.2 %copy-start.5 = (s32[32]{0:T(128)S(1)}, s32[32]{0:T(128)}, u32[]{:S(2)}) copy-start(s32[32]{0:T(128)} %param.15) | copy-start | bytes 388
Sparse Core Ops, SparseCore 0:
  9.5 48.3 all-gather.3
